TPU v7x, 512 devices: a whole 4x8x8 slice. The times are simulated.
512 devices in a mesh: af: 16 (over z, core), gy: 4 (over x), gz: 8 (over y).
Axes of the slice: x: 4, y: 8, z: 8, core: 2. Of those that a mesh axis runs over, the one named last changes fastest.
Arguments:
- slab: bfloat16 [512, 262144], P('af', ('gy', 'gz')), may hold values from -4000 to 4000
- block_owner: int32 [4, 8, 16], P('gy', 'gz'), may hold values from 0 to 15, each once within a row
- basis_init: float32 [512, 128], replicated, may hold values from -0.25 to 0.25
Outputs:
- triangle: float32 [512, 512], replicated
- basis: float32 [512, 128], replicated
- core: bfloat16 [128, 262144], P(None, ('gy', 'gz', 'af'))
Inputs may be any that keep to these rules, and one draw needn't show every extreme that they name: For every gy and gz index, block_owner[gy, gz, :] is a permutation of the 16 af indices.
All inputs are finite; a program needn't handle non-finite values.
Results may differ from a plain program's by a relative error of at most 0.0049.
Values may be sent and summed in bfloat16 or wider, within the bound.
A program may use at most 64 MiB of HBM per device.

v0:
```python
import jax
import jax.numpy as jnp
from jax import lax
from jax.sharding import PartitionSpec as P

ITERS = 2
exact_mode = lax.Precision.HIGHEST


def orthonormal(matrix):
    inner_prod = jnp.dot(matrix.T, matrix, precision=exact_mode)
    factor = jnp.linalg.cholesky(inner_prod)
    return lax.linalg.triangular_solve(
        factor, matrix, left_side=False, lower=True, transpose_a=True
    )


def on_device(slab, block_owner, basis_init):
    fibers = lax.axis_size("af")
    local_rows = slab.shape[0]
    block_cols = slab.shape[1] // fibers
    owners = block_owner.reshape(fibers)
    labels = jnp.arange(fibers, dtype=jnp.int32)
    onehot = (owners[:, None] == labels[None, :]).astype(jnp.int32)
    source = jnp.sum(onehot * labels[:, None], axis=0)
    pieces = slab.reshape(local_rows, fibers, block_cols)
    arranged = jnp.take(pieces, source, axis=1)
    received = lax.all_to_all(arranged, "af", split_axis=1, concat_axis=0, tiled=True)
    columns = received.reshape(local_rows * fibers, block_cols)
    devices_all = fibers * lax.axis_size("gy") * lax.axis_size("gz")
    divisor = block_cols * devices_all
    gram_local = (
        lax.dot_general(
            columns, columns, (((1,), (1,)), ((), ())), preferred_element_type=jnp.float32
        )
        / divisor
    )
    summed = lax.psum(gram_local, ("af", "gy", "gz"))
    triangle = jnp.linalg.cholesky(summed)
    basis = basis_init
    for sweep in range(ITERS):
        half_basis = orthonormal(jnp.dot(triangle.T, basis, precision=exact_mode))
        basis = orthonormal(jnp.dot(triangle, half_basis, precision=exact_mode))
    narrow = basis.astype(jnp.bfloat16)
    core = jnp.dot(narrow.T, columns, preferred_element_type=jnp.float32).astype(jnp.bfloat16)
    return (triangle, basis, core)


def solution(mesh):
    placed = (P("af", ("gy", "gz")), P("gy", "gz", None), P())
    return jax.shard_map(
        on_device,
        mesh=mesh,
        in_specs=placed,
        out_specs=(P(), P(), P(None, ("gy", "gz", "af"))),
        check_vma=False,
    )
```

profile of v0, /device:TPU:23, one launch (start us, length us, event | category | flops | bytes accessed | tf_op | source)
XLA Modules:
  0.0 510.2 jit_solution(9935144710232852774)
XLA Ops:
  7.2 0.6 copy-done.5
  8.0 1.1 copy.39
  9.1 0.6 gather_fusion
  9.8 28.0 %all_to_all.15 = bf16[32,16,512]{2,0,1:T(8,128)(2,1)S(1)} all-to-all(bf16[32,16,512]{2,0,1:T(8,128)(2,1)S(1)} %select_bitcast_fusion), channel_id=1, replica_groups=mesh['af'=16,'gy'=4,'gz'=8] {'af'}, dimensions={1} | all-to-all | bytes 1048576 | tf_op jit(solution)/shard_map/all_to_all | solution.py:28
  37.8 1.4 convolution_multiply_fusion
  39.3 273.1 %all-reduce.3.cloned.1.call-done = f32[512,512]{0,1:T(8,128)} async-done(((f32[512,512]{0,1:T(8,128)}), f32[512,512]{0,1:T(8,128)}) %all-reduce.3.cloned.1.call-update) | async-done | bytes 1048592 | tf_op jit(solution)/shard_map/psum | solution.py:38
  312.4 1.6 copy.30
  314.3 1.0 copy-done.3
  315.3 11.7 %cholesky.120 = f32[128,128]{1,0:T(8,128)S(1)} custom-call(f32[128,128]{1,0:T(8,128)S(1)} %cholesky.382), custom_call_target="Cholesky" | custom-call | tf_op jit(solution)/shard_map/jit(cholesky)/cholesky | solution.py:39
  327.1 9.8 %custom-call.32 = f32[1,128,128]{1,2,0:T(8,128)S(1)} custom-call(f32[1,128,128]{2,1,0:T(8,128)S(1)} %get-tuple-element.26), custom_call_target="InvertDiagBlocksLowerTriangular" | custom-call | tf_op jit(solution)/shard_map/jit(cholesky)/cholesky | solution.py:39
  337.7 11.7 %cholesky.244 = f32[128,128]{1,0:T(8,128)S(1)} custom-call(f32[128,128]{1,0:T(8,128)S(1)} %cholesky.386), custom_call_target="Cholesky" | custom-call | tf_op jit(solution)/shard_map/jit(cholesky)/cholesky | solution.py:39
  349.4 10.1 %custom-call.33 = f32[1,128,128]{1,2,0:T(8,128)S(1)} custom-call(f32[1,128,128]{2,1,0:T(8,128)S(1)} %get-tuple-element.23), custom_call_target="InvertDiagBlocksLowerTriangular" | custom-call | tf_op jit(solution)/shard_map/jit(cholesky)/cholesky | solution.py:39
  360.2 11.7 %cholesky.265 = f32[128,128]{1,0:T(8,128)S(1)} custom-call(f32[128,128]{1,0:T(8,128)S(1)} %cholesky.391), custom_call_target="Cholesky" | custom-call | tf_op jit(solution)/shard_map/jit(cholesky)/cholesky | solution.py:39
  372.0 0.6 compare_reduce_fusion.5
  372.6 9.8 %custom-call.34 = f32[1,128,128]{1,2,0:T(8,128)S(1)} custom-call(f32[1,128,128]{2,1,0:T(8,128)S(1)} %get-tuple-element.20), custom_call_target="InvertDiagBlocksLowerTriangular" | custom-call | tf_op jit(solution)/shard_map/jit(cholesky)/cholesky | solution.py:39
  383.0 11.9 %cholesky.282 = f32[128,128]{1,0:T(8,128)S(1)} custom-call(f32[128,128]{1,0:T(8,128)S(1)} %convolution_subtract_fusion.2), custom_call_target="Cholesky" | custom-call | tf_op jit(solution)/shard_map/jit(cholesky)/cholesky | solution.py:39
  394.9 0.7 compare_reduce_fusion.4
  395.7 0.6 compare_reduce_fusion.6
  399.1 1.8 fusion.26
  400.9 0.6 fusion.27
  401.6 11.7 %cholesky.340 = f32[128,128]{1,0:T(8,128)S(1)} custom-call(f32[128,128]{1,0:T(8,128)S(1)} %fusion.21), custom_call_target="Cholesky" | custom-call | tf_op jit(solution)/shard_map/jit(cholesky)/cholesky | solution.py:12
  413.4 0.6 compare_reduce_fusion.3
  414.0 0.7 fusion.8
  414.7 9.8 %custom-call.38 = f32[1,128,128]{1,2,0:T(8,128)S(1)} custom-call(f32[1,128,128]{2,1,0:T(8,128)S(1)} %fusion.8), custom_call_target="InvertDiagBlocksLowerTriangular" | custom-call | tf_op jit(solution)/shard_map/triangular_solve/custom-call.8 | solution.py:13
  424.5 0.4 convolution_bitcast_fusion.3
  424.9 1.0 fusion.28
  425.9 0.6 fusion.29
  426.6 11.9 %cholesky.351 = f32[128,128]{1,0:T(8,128)S(1)} custom-call(f32[128,128]{1,0:T(8,128)S(1)} %fusion.19), custom_call_target="Cholesky" | custom-call | tf_op jit(solution)/shard_map/jit(cholesky)/cholesky | solution.py:12
  438.6 0.6 compare_reduce_fusion.2
  439.2 0.7 fusion.9
  439.9 9.8 %custom-call.39 = f32[1,128,128]{1,2,0:T(8,128)S(1)} custom-call(f32[1,128,128]{2,1,0:T(8,128)S(1)} %fusion.9), custom_call_target="InvertDiagBlocksLowerTriangular" | custom-call | tf_op jit(solution)/shard_map/triangular_solve/custom-call.8 | solution.py:13
  449.7 0.4 convolution_bitcast_fusion.2
  450.1 1.8 fusion.30
  451.9 0.6 fusion.31
  452.6 11.7 %cholesky.362 = f32[128,128]{1,0:T(8,128)S(1)} custom-call(f32[128,128]{1,0:T(8,128)S(1)} %fusion.17), custom_call_target="Cholesky" | custom-call | tf_op jit(solution)/shard_map/jit(cholesky)/cholesky | solution.py:12
  464.4 0.6 compare_reduce_fusion.1
  465.0 0.7 fusion.10
  465.7 10.0 %custom-call.40 = f32[1,128,128]{1,2,0:T(8,128)S(1)} custom-call(f32[1,128,128]{2,1,0:T(8,128)S(1)} %fusion.10), custom_call_target="InvertDiagBlocksLowerTriangular" | custom-call | tf_op jit(solution)/shard_map/triangular_solve/custom-call.8 | solution.py:13
  475.7 0.4 convolution_bitcast_fusion.1
  476.1 1.0 fusion.32
  477.1 0.6 fusion.33
  477.8 11.7 %cholesky.373 = f32[128,128]{1,0:T(8,128)S(1)} custom-call(f32[128,128]{1,0:T(8,128)S(1)} %fusion.15), custom_call_target="Cholesky" | custom-call | tf_op jit(solution)/shard_map/jit(cholesky)/cholesky | solution.py:12
  489.6 0.6 compare_reduce_fusion
  490.2 0.7 fusion.11
  490.9 9.8 %custom-call.41 = f32[1,128,128]{1,2,0:T(8,128)S(1)} custom-call(f32[1,128,128]{2,1,0:T(8,128)S(1)} %fusion.11), custom_call_target="InvertDiagBlocksLowerTriangular" | custom-call | tf_op jit(solution)/shard_map/triangular_solve/custom-call.8 | solution.py:13
  500.7 0.4 convolution_bitcast_fusion
  501.1 0.9 convolution_convert_fusion
  502.0 0.8 copy.35
  (45 shorter events, 3.4 us)
Async XLA Ops:
  7.2 391.9 %copy-start = (f32[512,128]{1,0:T(8,128)S(1)}, f32[512,128]{1,0:T(8,128)}, u32[]{:S(2)}) copy-start(f32[512,128]{1,0:T(8,128)} %param.8) | copy-start | bytes 786436
  7.2 0.7 copy-start.5
  7.2 305.2 %all-reduce.3.cloned.1.call-start = ((), (), s32[]{:S(2)}) async-start(), calls=%async_computation.1 | async-start | bytes 2097152 | tf_op jit(solution)/shard_map/psum | solution.py:38
  312.4 1.7 copy-start.2
  314.3 1.0 copy-start.3
  315.3 21.7 %copy-start.4 = (f32[512,512]{1,0:T(8,128)S(1)}, f32[512,512]{1,0:T(8,128)}, u32[]{:S(2)}) copy-start(f32[512,512]{1,0:T(8,128)} %copy-done.3) | copy-start | bytes 3145732
  399.1 77.1 %copy-start.1 = (f32[512,512]{1,0:T(8,128)}, f32[512,512]{1,0:T(8,128)S(1)}, u32[]{:S(2)}) copy-start(f32[512,512]{1,0:T(8,128)S(1)} %select_select_fusion) | copy-start | bytes 3145732
Sparse Core Ops, SparseCore 0:
  39.4 272.9 all-reduce.2
where the time goes:
time: 519 us; the launch traced here: 510 us
  waiting for transfers between devices  273 us (53%)
  other arithmetic  171 us (33%)
  blocking collectives  28 us (5%)
  between operations  17.5 us (3%)
  matrix products  13.8 us (3%)
  local copies, waits for them, and re-layouts  6.28 us (1%)
    psum x1, waiting for transfers between devices, on_device(): summed = lax.psum(gram_local, ('af', 'gy', 'gz'))  273 us
    another operation x14, other arithmetic, on_device(): triangle = jnp.linalg.cholesky(summed)  78.9 us
    another operation x12, other arithmetic, orthonormal(): factor = jnp.linalg.cholesky(inner_prod)  49.8 us
    another operation x8, other arithmetic, orthonormal(): lax.linalg.triangular_solve(factor, matrix, left_side=False, lower=True,...  42.1 us
    all_to_all x1, blocking collectives, on_device(): lax.all_to_all(arranged, 'af', split_axis=1, concat_axis=0, tiled=True)  28 us
  transfers between devices with their start and end apart: 1, of which 1 were waited for; matrix products, arithmetic and copies ran while one was open for 0% of the time, Pallas kernels for 0%

commit v1 on v0

--- a/solution.py
+++ b/solution.py
@@ -35,7 +35,7 @@
         )
         / divisor
     )
-    summed = lax.psum(gram_local, ("af", "gy", "gz"))
+    summed = lax.psum(lax.psum(gram_local, ("gy", "gz")), "af")
     triangle = jnp.linalg.cholesky(summed)
     basis = basis_init
     for sweep in range(ITERS):

time: 519 us -> 523 us (level)
  the two profiles are of different devices: /device:TPU:23 before, /device:TPU:1 now
where the time goes in v1:
time: 523 us; the launch traced here: 514 us
  waiting for transfers between devices  276 us (53%)
  other arithmetic  171 us (33%)
  blocking collectives  28.8 us (6%)
  between operations  17.5 us (3%)
  matrix products  13.8 us (3%)
  local copies, waits for them, and re-layouts  6.28 us (1%)
    psum x2, waiting for transfers between devices, on_device(): summed = lax.psum(lax.psum(gram_local, ('gy', 'gz')), 'af')  276 us
    another operation x14, other arithmetic, on_device(): triangle = jnp.linalg.cholesky(summed)  78.7 us
    another operation x12, other arithmetic, orthonormal(): factor = jnp.linalg.cholesky(inner_prod)  49.8 us
    another operation x8, other arithmetic, orthonormal(): lax.linalg.triangular_solve(factor, matrix, left_side=False, lower=True,...  42.1 us
    all_to_all x1, blocking collectives, on_device(): lax.all_to_all(arranged, 'af', split_axis=1, concat_axis=0, tiled=True)  28.8 us
  transfers between devices with their start and end apart: 2, of which 2 were waited for; matrix products, arithmetic and copies ran while one was open for 0% of the time, Pallas kernels for 0%

profile of v1, /device:TPU:1, one launch (start us, length us, event | category | flops | bytes accessed | tf_op | source)
XLA Modules:
  0.0 514.2 jit_solution(5079108620588426243)
XLA Ops:
  7.2 0.6 copy-done.5
  8.0 1.1 copy.39
  9.1 0.6 gather_fusion
  9.8 28.8 %all_to_all.15 = bf16[32,16,512]{2,0,1:T(8,128)(2,1)S(1)} all-to-all(bf16[32,16,512]{2,0,1:T(8,128)(2,1)S(1)} %select_bitcast_fusion), channel_id=1, replica_groups=mesh['af'=16,'gy'=4,'gz'=8] {'af'}, dimensions={1} | all-to-all | bytes 1048576 | tf_op jit(solution)/shard_map/all_to_all | solution.py:28
  38.6 1.4 convolution_multiply_fusion
  40.1 153.2 %all-reduce.4.cloned.1.call-done = f32[512,512]{0,1:T(8,128)} async-done(((f32[512,512]{0,1:T(8,128)}), f32[512,512]{0,1:T(8,128)}) %all-reduce.4.cloned.1.call-update) | async-done | bytes 1048592 | tf_op jit(solution)/shard_map/psum | solution.py:38
  193.4 123.1 %all-reduce.6.cloned.1.call-done = f32[512,512]{0,1:T(8,128)} async-done(((f32[512,512]{0,1:T(8,128)}), f32[512,512]{0,1:T(8,128)}) %all-reduce.6.cloned.1.call-update) | async-done | bytes 1048592 | tf_op jit(solution)/shard_map/psum | solution.py:38
  316.4 1.6 copy.30
  318.4 1.0 copy-done.3
  319.3 11.7 %cholesky.120 = f32[128,128]{1,0:T(8,128)S(1)} custom-call(f32[128,128]{1,0:T(8,128)S(1)} %cholesky.382), custom_call_target="Cholesky" | custom-call | tf_op jit(solution)/shard_map/jit(cholesky)/cholesky | solution.py:39
  331.1 9.8 %custom-call.32 = f32[1,128,128]{1,2,0:T(8,128)S(1)} custom-call(f32[1,128,128]{2,1,0:T(8,128)S(1)} %get-tuple-element.26), custom_call_target="InvertDiagBlocksLowerTriangular" | custom-call | tf_op jit(solution)/shard_map/jit(cholesky)/cholesky | solution.py:39
  341.7 11.7 %cholesky.244 = f32[128,128]{1,0:T(8,128)S(1)} custom-call(f32[128,128]{1,0:T(8,128)S(1)} %cholesky.386), custom_call_target="Cholesky" | custom-call | tf_op jit(solution)/shard_map/jit(cholesky)/cholesky | solution.py:39
  353.5 10.1 %custom-call.33 = f32[1,128,128]{1,2,0:T(8,128)S(1)} custom-call(f32[1,128,128]{2,1,0:T(8,128)S(1)} %get-tuple-element.23), custom_call_target="InvertDiagBlocksLowerTriangular" | custom-call | tf_op jit(solution)/shard_map/jit(cholesky)/cholesky | solution.py:39
  364.3 11.7 %cholesky.265 = f32[128,128]{1,0:T(8,128)S(1)} custom-call(f32[128,128]{1,0:T(8,128)S(1)} %cholesky.391), custom_call_target="Cholesky" | custom-call | tf_op jit(solution)/shard_map/jit(cholesky)/cholesky | solution.py:39
  376.0 0.6 compare_reduce_fusion.5
  376.6 9.8 %custom-call.34 = f32[1,128,128]{1,2,0:T(8,128)S(1)} custom-call(f32[1,128,128]{2,1,0:T(8,128)S(1)} %get-tuple-element.20), custom_call_target="InvertDiagBlocksLowerTriangular" | custom-call | tf_op jit(solution)/shard_map/jit(cholesky)/cholesky | solution.py:39
  387.1 11.7 %cholesky.282 = f32[128,128]{1,0:T(8,128)S(1)} custom-call(f32[128,128]{1,0:T(8,128)S(1)} %convolution_subtract_fusion.2), custom_call_target="Cholesky" | custom-call | tf_op jit(solution)/shard_map/jit(cholesky)/cholesky | solution.py:39
  398.8 0.7 compare_reduce_fusion.4
  399.5 0.6 compare_reduce_fusion.6
  403.1 1.8 fusion.26
  404.9 0.6 fusion.27
  405.6 11.7 %cholesky.340 = f32[128,128]{1,0:T(8,128)S(1)} custom-call(f32[128,128]{1,0:T(8,128)S(1)} %fusion.21), custom_call_target="Cholesky" | custom-call | tf_op jit(solution)/shard_map/jit(cholesky)/cholesky | solution.py:12
  417.4 0.6 compare_reduce_fusion.3
  418.0 0.7 fusion.8
  418.7 9.8 %custom-call.38 = f32[1,128,128]{1,2,0:T(8,128)S(1)} custom-call(f32[1,128,128]{2,1,0:T(8,128)S(1)} %fusion.8), custom_call_target="InvertDiagBlocksLowerTriangular" | custom-call | tf_op jit(solution)/shard_map/triangular_solve/custom-call.8 | solution.py:13
  428.5 0.4 convolution_bitcast_fusion.3
  428.9 1.0 fusion.28
  429.9 0.6 fusion.29
  430.6 11.9 %cholesky.351 = f32[128,128]{1,0:T(8,128)S(1)} custom-call(f32[128,128]{1,0:T(8,128)S(1)} %fusion.19), custom_call_target="Cholesky" | custom-call | tf_op jit(solution)/shard_map/jit(cholesky)/cholesky | solution.py:12
  442.6 0.6 compare_reduce_fusion.2
  443.2 0.7 fusion.9
  443.9 9.8 %custom-call.39 = f32[1,128,128]{1,2,0:T(8,128)S(1)} custom-call(f32[1,128,128]{2,1,0:T(8,128)S(1)} %fusion.9), custom_call_target="InvertDiagBlocksLowerTriangular" | custom-call | tf_op jit(solution)/shard_map/triangular_solve/custom-call.8 | solution.py:13
  453.7 0.4 convolution_bitcast_fusion.2
  454.1 1.8 fusion.30
  455.9 0.6 fusion.31
  456.6 11.7 %cholesky.362 = f32[128,128]{1,0:T(8,128)S(1)} custom-call(f32[128,128]{1,0:T(8,128)S(1)} %fusion.17), custom_call_target="Cholesky" | custom-call | tf_op jit(solution)/shard_map/jit(cholesky)/cholesky | solution.py:12
  468.4 0.6 compare_reduce_fusion.1
  469.0 0.7 fusion.10
  469.7 10.0 %custom-call.40 = f32[1,128,128]{1,2,0:T(8,128)S(1)} custom-call(f32[1,128,128]{2,1,0:T(8,128)S(1)} %fusion.10), custom_call_target="InvertDiagBlocksLowerTriangular" | custom-call | tf_op jit(solution)/shard_map/triangular_solve/custom-call.8 | solution.py:13
  480.2 1.0 fusion.32
  481.2 0.6 fusion.33
  481.9 11.7 %cholesky.373 = f32[128,128]{1,0:T(8,128)S(1)} custom-call(f32[128,128]{1,0:T(8,128)S(1)} %fusion.15), custom_call_target="Cholesky" | custom-call | tf_op jit(solution)/shard_map/jit(cholesky)/cholesky | solution.py:12
  493.6 0.6 compare_reduce_fusion
  494.3 0.7 fusion.11
  494.9 9.8 %custom-call.41 = f32[1,128,128]{1,2,0:T(8,128)S(1)} custom-call(f32[1,128,128]{2,1,0:T(8,128)S(1)} %fusion.11), custom_call_target="InvertDiagBlocksLowerTriangular" | custom-call | tf_op jit(solution)/shard_map/triangular_solve/custom-call.8 | solution.py:13
  504.7 0.4 convolution_bitcast_fusion
  505.2 0.9 convolution_convert_fusion
  506.1 0.8 copy.35
  (48 shorter events, 4.0 us)
Async XLA Ops:
  7.2 395.9 %copy-start = (f32[512,128]{1,0:T(8,128)S(1)}, f32[512,128]{1,0:T(8,128)}, u32[]{:S(2)}) copy-start(f32[512,128]{1,0:T(8,128)} %param.8) | copy-start | bytes 786436
  7.2 0.7 copy-start.5
  7.2 186.1 %all-reduce.4.cloned.1.call-start = ((), (), s32[]{:S(2)}) async-start(), calls=%async_computation.1 | async-start | bytes 2097152 | tf_op jit(solution)/shard_map/psum | solution.py:38
  40.1 276.3 %all-reduce.6.cloned.1.call-start = ((), (), s32[]{:S(2)}) async-start(), calls=%async_computation.2 | async-start | bytes 2097152 | tf_op jit(solution)/shard_map/psum | solution.py:38
  316.4 1.7 copy-start.2
  318.3 1.0 copy-start.3
  319.3 21.7 %copy-start.4 = (f32[512,512]{1,0:T(8,128)S(1)}, f32[512,512]{1,0:T(8,128)}, u32[]{:S(2)}) copy-start(f32[512,512]{1,0:T(8,128)} %copy-done.3) | copy-start | bytes 3145732
  403.1 77.1 %copy-start.1 = (f32[512,512]{1,0:T(8,128)}, f32[512,512]{1,0:T(8,128)S(1)}, u32[]{:S(2)}) copy-start(f32[512,512]{1,0:T(8,128)S(1)} %select_select_fusion) | copy-start | bytes 3145732
Sparse Core Ops, SparseCore 0:
  40.2 153.0 all-reduce.3
  195.7 120.7 all-reduce.5
